TPU v7x, 32 devices: a whole 2x2x4 slice. The times are simulated.
32 devices in a mesh: blk: 2 (over x), rows: 16 (over z, y, core).
Axes of the slice: x: 2, y: 2, z: 4, core: 2. Of those that a mesh axis runs over, the one named last changes fastest.
Arguments:
- features: bfloat16 [8192, 128], P(('blk', 'rows')), may hold values from -6 to 6
- labels: int32 [8192], P(('blk', 'rows')), may hold values from 0 to 6
- destination: int32 [8192, 1], P(('blk', 'rows')), may hold values from 0 to 15; in each aligned block of 256 rows (0 to 255, 256 to 511, ...) at most 32 rows name the same one
- centres: bfloat16 [8192, 128], P('blk'), may hold values from -6 to 6
- tri_inverse: float32 [8192, 8192], P('blk', 'rows'), may hold values from -1 to 2, as said below
- aux_inverse: float32 [8192, 8192], P('blk', 'rows'), may hold values from -1 to 2, as said below
Outputs:
- predictions: float32 [7, 16384], P(None, ('blk', 'rows'))
Inputs may be any that keep to these rules, and one draw needn't show every extreme that they name: `destination`: in each aligned block of 256 rows (the rows of one device) no value occurs more than 32 times, and some value occurs exactly 32 times. `tri_inverse`: zero below the diagonal, positive on it. `aux_inverse`: zero below the diagonal, positive on it.
All inputs are finite; a program needn't handle non-finite values.
Results may differ from a plain program's by a relative error of at most 0.0003.
Values may be sent and summed in bfloat16 or wider, within the bound.
A program may use at most 128 MiB of HBM per device.

v0:
```python
import math
import jax
import jax.numpy as jnp
from jax import lax
from jax.sharding import PartitionSpec as P

M = 8192
CLASSES = 7
ITERS = 2
ridge_weight = 0.1
highest = lax.Precision.HIGHEST


def vector_total(values):
    return lax.psum(values, ("blk", "rows"))


def square_norms(rows_x):
    return jnp.einsum("nd,nd->n", rows_x, rows_x, preferred_element_type=jnp.float32)


def kernel_tile(rows_x, rows_norm, centre_x, centre_norm, scale):
    inner = lax.dot_general(
        rows_x, centre_x, (((1,), (1,)), ((), ())), preferred_element_type=jnp.float32
    )
    return jnp.exp(-(rows_norm[:, None] + centre_norm[None, :] - 2.0 * inner) * scale).astype(
        jnp.bfloat16
    )


def against_rows(vector_low, tile):
    return lax.dot_general(
        vector_low, tile, (((1,), (1,)), ((), ())), preferred_element_type=jnp.float32
    )


def factor_forward(block, vector):
    block_rows, block_cols = block.shape
    ours = lax.dynamic_slice_in_dim(vector, lax.axis_index("rows") * block_cols, block_cols, 1)
    partial_rows = lax.dot_general(
        ours, block, (((1,), (1,)), ((), ())), precision=highest, preferred_element_type=jnp.float32
    )
    summed = lax.psum(partial_rows, "rows")
    return lax.all_gather(summed, "blk", axis=1, tiled=True)


def factor_backward(block, vector):
    block_rows, block_cols = block.shape
    ours = lax.dynamic_slice_in_dim(vector, lax.axis_index("blk") * block_rows, block_rows, 1)
    partial_cols = jnp.dot(ours, block, precision=highest, preferred_element_type=jnp.float32)
    summed = lax.psum(partial_cols, "blk")
    return lax.all_gather(summed, "rows", axis=1, tiled=True)


def class_targets(tags):
    class_ids = jnp.arange(CLASSES, dtype=jnp.float32)[:, None] + 1.0
    live = (tags > 0.5).astype(jnp.float32)
    return (live, live[None, :] * jnp.where(tags[None, :] == class_ids, 1.0, -1.0))


def on_device(features, labels, destination, centres, tri_inverse, aux_inverse):
    groups = lax.axis_size("rows")
    own_rows, width = features.shape
    capacity = max(2, 2 * own_rows // groups)
    scale = 2.0 / width
    count_all = float(own_rows * lax.axis_size("blk") * groups)
    target = destination[:, 0]
    picks = (target[:, None] == jnp.arange(groups, dtype=jnp.int32)[None, :]).astype(jnp.int32)
    before = jnp.sum((jnp.cumsum(picks, axis=0) - picks) * picks, axis=1)
    send_rows = jnp.zeros((groups, capacity, width), jnp.bfloat16).at[target, before].set(features)
    send_tags = (
        jnp.zeros((groups, capacity), jnp.bfloat16)
        .at[target, before]
        .set((labels + 1).astype(jnp.bfloat16))
    )
    got_rows, got_tags = (
        lax.all_to_all(send_rows, "rows", split_axis=0, concat_axis=0, tiled=True),
        lax.all_to_all(send_tags, "rows", split_axis=0, concat_axis=0, tiled=True),
    )
    slots = groups * capacity
    slot_rows = got_rows.reshape(slots, width)
    slot_tags = got_tags.reshape(slots)
    live, targets = class_targets(slot_tags.astype(jnp.float32))
    every_centre = lax.all_gather(centres, "blk", axis=0, tiled=True)
    centre_norm = square_norms(every_centre)
    block_rows = math.gcd(slots, 64)
    block_count = slots // block_rows
    stacked_rows = slot_rows.reshape(block_count, block_rows, width)
    stacked_live = live.reshape(block_count, block_rows)
    stacked_targets = (
        targets.astype(jnp.bfloat16).reshape(CLASSES, block_count, block_rows).transpose(1, 0, 2)
    )

    def tile_of(rows_x):
        return kernel_tile(rows_x, square_norms(rows_x), every_centre, centre_norm, scale)

    def gram_apply(vector):
        vector_low = vector.astype(jnp.bfloat16)

        def gram_visit(carry, pieces):
            rows_x, rows_live = pieces
            tile = tile_of(rows_x)
            image = (against_rows(vector_low, tile) * rows_live[None, :]).astype(jnp.bfloat16)
            return (carry + jnp.dot(image, tile, preferred_element_type=jnp.float32), None)

        partial_sum, _ = lax.scan(
            gram_visit, jnp.zeros((CLASSES, M), jnp.float32), (stacked_rows, stacked_live)
        )
        return vector_total(partial_sum) / count_all

    def kernel_visit(carry, pieces):
        rows_x, rows_targets = pieces
        return (
            carry + jnp.dot(rows_targets, tile_of(rows_x), preferred_element_type=jnp.float32),
            None,
        )

    partial_sum, _ = lax.scan(
        kernel_visit, jnp.zeros((CLASSES, M), jnp.float32), (stacked_rows, stacked_targets)
    )
    rhs = factor_backward(
        aux_inverse, factor_backward(tri_inverse, vector_total(partial_sum) / count_all)
    )
    solution = jnp.zeros((CLASSES, M), jnp.float32)
    residual = rhs
    direction = rhs
    norm_now = jnp.sum(residual * residual, axis=1, keepdims=True)
    for step in range(ITERS):
        first = factor_forward(aux_inverse, direction)
        second = factor_forward(tri_inverse, first)
        third = factor_backward(tri_inverse, gram_apply(second))
        image = factor_backward(aux_inverse, third + ridge_weight * first)
        step_size = norm_now / jnp.sum(direction * image, axis=1, keepdims=True)
        solution = solution + step_size * direction
        residual = residual - step_size * image
        norm_next = jnp.sum(residual * residual, axis=1, keepdims=True)
        direction = residual + norm_next / norm_now * direction
        norm_now = norm_next
    coefficients = factor_forward(tri_inverse, factor_forward(aux_inverse, solution))
    vector_low = coefficients.astype(jnp.bfloat16)
    scores = lax.map(lambda rows_x: against_rows(vector_low, tile_of(rows_x)), stacked_rows)
    return scores.transpose(1, 0, 2).reshape(CLASSES, slots) * live[None, :]


def solution(mesh):
    return jax.shard_map(
        on_device,
        mesh=mesh,
        in_specs=(
            P(("blk", "rows"), None),
            P(("blk", "rows")),
            P(("blk", "rows"), None),
            P("blk", None),
            P("blk", "rows"),
            P("blk", "rows"),
        ),
        out_specs=P(None, ("blk", "rows")),
        check_vma=False,
    )
```

profile of v0, /device:TPU:0, one launch (start us, length us, event | category | flops | bytes accessed | tf_op | source)
XLA Modules:
  0.0 1247.6 jit_solution(15171571763644554743)
XLA Ops:
  10.9 12.9 %scatter_fusion.1 = bf16[16,32]{1,0:T(8,128)(2,1)S(1)} fusion(bf16[16,32]{1,0:T(8,128)(2,1)S(1)} %broadcast_in_dim.21, s32[256]{0:T(256)S(1)} %bitcast.127, bf16[256]{0:T(256)(128)(2,1)S(1)} %add_convert_fusion), kind=kCustom, calls=%fused_computation.1 | custom fusion | bytes 3584 | tf_op jit(solution)/shard_map/scatter | solution.py:74
  24.5 7.4 all-to-all-start.1
  32.5 27.0 %scatter_fusion = bf16[16,32,128]{2,1,0:T(8,128)(2,1)} fusion(bf16[16,32,128]{2,1,0:T(8,128)(2,1)} %broadcast_in_dim.20, s32[256]{0:T(256)S(1)} %bitcast.128, bf16[256,128]{1,0:T(8,128)(2,1)S(1)} %copy-done.5), kind=kCustom, calls=%fused_computation | custom fusion | bytes 198656 | tf_op jit(solution)/shard_map/scatter | solution.py:70
  59.5 5.8 all-to-all-start
  65.6 2.9 fusion.63
  68.5 4.8 all-to-all-done
  73.3 9.2 while.44
  83.3 122.6 %all-reduce.7.cloned.1.call-done = f32[7,8192]{1,0:T(8,128)} async-done(((f32[7,8192]{1,0:T(8,128)}), f32[7,8192]{1,0:T(8,128)}) %all-reduce.7.cloned.1.call-update) | async-done | bytes 229392 | tf_op jit(solution)/shard_map/psum | solution.py:15
  205.9 5.7 fusion.68
  211.6 8.1 psum.106
  219.8 20.1 %all_gather.40 = f32[7,8192]{1,0:T(8,128)S(1)} all-gather(f32[7,512]{1,0:T(8,128)S(1)} %psum.106), channel_id=1, replica_groups=mesh['blk'=2,'rows'=16] {'rows'}, dimensions={1}, use_global_device_ids=true | all-gather | bytes 243712 | tf_op jit(solution)/shard_map/all_gather | solution.py:52
  239.9 5.7 fusion.69
  245.6 8.1 psum.107
  253.6 17.8 %all_gather.41 = f32[7,8192]{1,0:T(8,128)S(1)} all-gather(f32[7,512]{1,0:T(8,128)S(1)} %psum.107), channel_id=1, replica_groups=mesh['blk'=2,'rows'=16] {'rows'}, dimensions={1}, use_global_device_ids=true | all-gather | bytes 243712 | tf_op jit(solution)/shard_map/all_gather | solution.py:52
  271.5 9.8 fusion.94
  281.4 85.0 %all-reduce.9.cloned.1.call-done = f32[7,4096]{1,0:T(8,128)} async-done(((f32[7,4096]{1,0:T(8,128)}), f32[7,4096]{1,0:T(8,128)}) %all-reduce.9.cloned.1.call-update) | async-done | bytes 114704 | tf_op jit(solution)/shard_map/psum | solution.py:43
  366.3 7.1 all_gather.42
  373.4 9.1 fusion.87
  382.5 58.7 %psum.109 = bf16[7,4096]{1,0:T(8,128)(2,1)S(1)} all-reduce(f32[7,4096]{1,0:T(8,128)S(1)} %fusion.87), channel_id=1, replica_groups=mesh['blk'=2,'rows'=16] {'rows'}, use_global_device_ids=true, to_apply=%region_12.13 | all-reduce | flops 28672 | bytes 172032 | tf_op jit(solution)/shard_map/psum | solution.py:43
  441.2 4.9 all_gather.43
  446.1 28.1 %while.45 = (s32[]{:T(128)}, f32[7,8192]{1,0:T(8,128)S(1)}, bf16[8,64,128]{2,1,0:T(8,128)(2,1)S(1)}, f32[8192]{0:T(1024)S(1)}, bf16[8192,128]{1,0:T(8,128)(2,1)}...) while((s32[]{:T(128)}, f32[7,8192]{1,0:T(8,128)S(1)}, ...), condition=%wide.region_14.15_spmd.clone, body=%wide.region_13.14_spmd.clone.sunk | while | flops 152183616 | bytes 4834931 | solution.py:106
  446.2 2.5 fusion.178
  449.8 2.5 fusion.178
  453.3 2.5 fusion.178
  456.8 2.5 fusion.178
  460.3 2.5 fusion.178
  463.8 2.5 fusion.178
  467.3 2.5 fusion.178
  475.0 122.3 %all-reduce.11.cloned.1.call-done = f32[7,8192]{1,0:T(8,128)} async-done(((f32[7,8192]{1,0:T(8,128)}), f32[7,8192]{1,0:T(8,128)}) %all-reduce.11.cloned.1.call-update) | async-done | bytes 229392 | tf_op jit(solution)/shard_map/psum | solution.py:15
  597.3 5.7 fusion.67
  603.0 8.1 psum.111
  611.1 20.1 %all_gather.44 = f32[7,8192]{1,0:T(8,128)S(1)} all-gather(f32[7,512]{1,0:T(8,128)S(1)} %psum.111), channel_id=1, replica_groups=mesh['blk'=2,'rows'=16] {'rows'}, dimensions={1}, use_global_device_ids=true | all-gather | bytes 243712 | tf_op jit(solution)/shard_map/all_gather | solution.py:52
  631.2 5.7 fusion.66
  636.9 8.1 psum.112
  645.0 17.8 %all_gather.45 = f32[7,8192]{1,0:T(8,128)S(1)} all-gather(f32[7,512]{1,0:T(8,128)S(1)} %psum.112), channel_id=1, replica_groups=mesh['blk'=2,'rows'=16] {'rows'}, dimensions={1}, use_global_device_ids=true | all-gather | bytes 243712 | tf_op jit(solution)/shard_map/all_gather | solution.py:52
  663.4 9.8 fusion.91
  673.3 85.0 %all-reduce.13.cloned.1.call-done = f32[7,4096]{1,0:T(8,128)} async-done(((f32[7,4096]{1,0:T(8,128)}), f32[7,4096]{1,0:T(8,128)}) %all-reduce.13.cloned.1.call-update) | async-done | bytes 114704 | tf_op jit(solution)/shard_map/psum | solution.py:43
  758.3 6.8 all_gather.46
  765.0 9.1 fusion.84
  774.2 58.7 %psum.114 = bf16[7,4096]{1,0:T(8,128)(2,1)S(1)} all-reduce(f32[7,4096]{1,0:T(8,128)S(1)} %fusion.84), channel_id=1, replica_groups=mesh['blk'=2,'rows'=16] {'rows'}, use_global_device_ids=true, to_apply=%region_21.22 | all-reduce | flops 28672 | bytes 172032 | tf_op jit(solution)/shard_map/psum | solution.py:43
  832.8 4.9 all_gather.47
  837.8 28.1 %while.46 = (s32[]{:T(128)}, f32[7,8192]{1,0:T(8,128)S(1)}, bf16[8,64,128]{2,1,0:T(8,128)(2,1)S(1)}, f32[8192]{0:T(1024)S(1)}, bf16[8192,128]{1,0:T(8,128)(2,1)}...) while((s32[]{:T(128)}, f32[7,8192]{1,0:T(8,128)S(1)}, ...), condition=%wide.region_23.24_spmd.clone, body=%wide.region_22.23_spmd.clone.sunk | while | flops 152183616 | bytes 4834931 | solution.py:106
  837.9 2.5 fusion.185
  841.4 2.5 fusion.185
  844.9 2.5 fusion.185
  848.4 2.5 fusion.185
  851.9 2.5 fusion.185
  855.5 2.5 fusion.185
  859.0 2.5 fusion.185
  862.5 2.5 fusion.185
  866.6 122.3 %all-reduce.15.cloned.1.call-done = f32[7,8192]{1,0:T(8,128)} async-done(((f32[7,8192]{1,0:T(8,128)}), f32[7,8192]{1,0:T(8,128)}) %all-reduce.15.cloned.1.call-update) | async-done | bytes 229392 | tf_op jit(solution)/shard_map/psum | solution.py:15
  988.9 5.7 fusion.65
  994.6 8.1 psum.116
  1002.7 20.1 %all_gather.48 = f32[7,8192]{1,0:T(8,128)S(1)} all-gather(f32[7,512]{1,0:T(8,128)S(1)} %psum.116), channel_id=1, replica_groups=mesh['blk'=2,'rows'=16] {'rows'}, dimensions={1}, use_global_device_ids=true | all-gather | bytes 243712 | tf_op jit(solution)/shard_map/all_gather | solution.py:52
  1022.9 5.7 fusion.64
  1028.6 8.1 psum.117
  1036.6 17.8 %all_gather.49 = f32[7,8192]{1,0:T(8,128)S(1)} all-gather(f32[7,512]{1,0:T(8,128)S(1)} %psum.117), channel_id=1, replica_groups=mesh['blk'=2,'rows'=16] {'rows'}, dimensions={1}, use_global_device_ids=true | all-gather | bytes 243712 | tf_op jit(solution)/shard_map/all_gather | solution.py:52
  1054.6 9.8 fusion.81
  1064.5 84.9 %all-reduce.17.cloned.1.call-done = f32[7,4096]{1,0:T(8,128)} async-done(((f32[7,4096]{1,0:T(8,128)}), f32[7,4096]{1,0:T(8,128)}) %all-reduce.17.cloned.1.call-update) | async-done | bytes 114704 | tf_op jit(solution)/shard_map/psum | solution.py:43
  1149.5 6.8 all_gather.50
  1156.3 9.3 fusion.79
  1165.6 58.7 %psum.119 = bf16[7,4096]{1,0:T(8,128)(2,1)S(1)} all-reduce(f32[7,4096]{1,0:T(8,128)S(1)} %fusion.79), channel_id=1, replica_groups=mesh['blk'=2,'rows'=16] {'rows'}, use_global_device_ids=true, to_apply=%region_29.30 | all-reduce | flops 28672 | bytes 172032 | tf_op jit(solution)/shard_map/psum | solution.py:43
  1224.2 4.9 all_gather.51
  1229.2 10.7 while.43
  (140 shorter events, 48.2 us)
Async XLA Ops:
  6.5 26.0 %copy-start.5 = (bf16[256,128]{1,0:T(8,128)(2,1)S(1)}, bf16[256,128]{1,0:T(8,128)(2,1)}, u32[]{:S(2)}) copy-start(bf16[256,128]{1,0:T(8,128)(2,1)} %param.14) | copy-start | bytes 196612
  6.5 59.1 %all-gather.2.cloned.1.call-start = ((), (), s32[]{:S(2)}) async-start(), calls=%async_computation.2 | async-start | bytes 3145728 | tf_op jit(solution)/shard_map/all_gather | solution.py:84
  24.5 35.1 %all-to-all-start.1 = ((bf16[16,1,32]{2,1,0:T(2,128)(2,1)}), bf16[16,1,32]{2,1,0:T(2,128)(2,1)S(1)}, u32[]{:S(2)}, u32[]{:S(2)}) async-start(bf16[16,1,32]{2,1,0:T(2,128)(2,1)} %copy.11), calls=%async_computation.1 | async-start | bytes 16384 | tf_op jit(solution)/shard_map/all_to_all | solution.py:78
  59.5 13.8 %all-to-all-start = ((bf16[16,32,128]{2,1,0:T(8,128)(2,1)}), bf16[16,32,128]{2,1,0:T(8,128)(2,1)S(1)}, u32[]{:S(2)}, u32[]{:S(2)}) async-start(bf16[16,32,128]{2,1,0:T(8,128)(2,1)} %scatter_fusion), calls=%async_computation | async-start | bytes 262144 | tf_op jit(solution)/shard_map/all_to_all | solution.py:77
  65.4 140.6 %all-reduce.7.cloned.1.call-start = ((), (), s32[]{:S(2)}) async-start(), calls=%async_computation.3 | async-start | bytes 524288 | tf_op jit(solution)/shard_map/psum | solution.py:15
  65.6 7.7 copy-start.2
  82.5 0.7 copy-start.4
  83.2 283.1 %all-reduce.9.cloned.1.call-start = ((), (), s32[]{:S(2)}) async-start(), calls=%async_computation.4 | async-start | bytes 262144 | tf_op jit(solution)/shard_map/psum | solution.py:43
  281.3 316.0 %all-reduce.11.cloned.1.call-start = ((), (), s32[]{:S(2)}) async-start(), calls=%async_computation.5 | async-start | bytes 524288 | tf_op jit(solution)/shard_map/psum | solution.py:15
  474.2 0.7 copy-start
  474.9 283.3 %all-reduce.13.cloned.1.call-start = ((), (), s32[]{:S(2)}) async-start(), calls=%async_computation.6 | async-start | bytes 262144 | tf_op jit(solution)/shard_map/psum | solution.py:43
  673.3 315.7 %all-reduce.15.cloned.1.call-start = ((), (), s32[]{:S(2)}) async-start(), calls=%async_computation.7 | async-start | bytes 524288 | tf_op jit(solution)/shard_map/psum | solution.py:15
  865.9 0.7 copy-start.1
  866.6 282.9 %all-reduce.17.cloned.1.call-start = ((), (), s32[]{:S(2)}) async-start(), calls=%async_computation.8 | async-start | bytes 262144 | tf_op jit(solution)/shard_map/psum | solution.py:43
  1156.3 72.9 %copy-start.3 = (bf16[8192,128]{1,0:T(8,128)(2,1)S(1)}, bf16[8192,128]{1,0:T(8,128)(2,1)}, u32[]{:S(2)}) copy-start(bf16[8192,128]{1,0:T(8,128)(2,1)} %get-tuple-element.545) | copy-start | bytes 6291460
Sparse Core Ops, SparseCore 0:
  8.9 35.8 all-gather.1
  83.4 122.5 all-reduce.6
  281.4 84.8 all-reduce.8
  475.1 122.1 all-reduce.10
  673.4 84.8 all-reduce.12
  866.7 122.1 all-reduce.14
  1064.6 84.8 all-reduce.16
where the time goes:
time: 1260 us; the launch traced here: 1250 us
  waiting for transfers between devices  628 us (50%)
  blocking collectives  374 us (30%)
  matrix products  163 us (13%)
  local copies, waits for them, and re-layouts  43.9 us (3%)
  between operations  13.9 us (1%)
  starting transfers between devices  13.5 us (1%)
    psum x3, waiting for transfers between devices, vector_total(): return lax.psum(values, ('blk', 'rows'))  367 us
    psum x3, waiting for transfers between devices, factor_forward(): summed = lax.psum(partial_rows, 'rows')  255 us
    psum x3, blocking collectives, factor_forward(): summed = lax.psum(partial_rows, 'rows')  176 us
    all_gather x6, blocking collectives, factor_backward(): return lax.all_gather(summed, 'rows', axis=1, tiled=True)  114 us
    dot_general x6, matrix products, factor_forward(): lax.dot_general(ours, block, (((1,), (1,)), ((), ())), precision=highest,...  57 us
    psum x6, blocking collectives, factor_backward(): summed = lax.psum(partial_cols, 'blk')  48.5 us
    dot_general x16, matrix products, kernel_tile(): lax.dot_general(rows_x, centre_x, (((1,), (1,)), ((), ())), preferred_ele...  39.3 us
    all_gather x6, blocking collectives, factor_forward(): return lax.all_gather(summed, 'blk', axis=1, tiled=True)  35.4 us
  transfers between devices with their start and end apart: 9, of which 7 were waited for; matrix products, arithmetic and copies ran while one was open for 4% of the time, Pallas kernels for 0%

commit v1 on v0

--- a/solution.py
+++ b/solution.py
@@ -11,8 +11,13 @@
 highest = lax.Precision.HIGHEST
 
 
+def by_each_axis(array, one, other):
+    half = lax.psum(array, one)
+    return lax.psum(half, other)
+
+
 def vector_total(values):
-    return lax.psum(values, ("blk", "rows"))
+    return by_each_axis(values, "rows", "blk")
 
 
 def square_norms(rows_x):

time: 1260 us -> 1230 us (0.976)
  waiting for transfers between devices: 628 us -> 597 us
    psum x3 -> x6, waiting for transfers between devices: 367 us -> 336 us  [the longest x3 259 us: by_each_axis(): half = lax.psum(array, one)]
  transfers between devices with their start and end apart: 9 -> 12, of which waited for: 7 -> 10; matrix products, arithmetic and copies ran while one was open for 4% -> 4% of each run, Pallas kernels for 0% -> 0%
where the time goes in v1:
time: 1230 us; the launch traced here: 1220 us
  waiting for transfers between devices  597 us (49%)
  blocking collectives  377 us (31%)
  matrix products  163 us (13%)
  local copies, waits for them, and re-layouts  43.9 us (4%)
  between operations  14 us (1%)
  starting transfers between devices  13.6 us (1%)
    psum x3, waiting for transfers between devices, by_each_axis(): half = lax.psum(array, one)  259 us
    psum x3, waiting for transfers between devices, factor_forward(): summed = lax.psum(partial_rows, 'rows')  255 us
    psum x3, blocking collectives, factor_forward(): summed = lax.psum(partial_rows, 'rows')  176 us
    all_gather x6, blocking collectives, factor_backward(): return lax.all_gather(summed, 'rows', axis=1, tiled=True)  121 us
    psum x3, waiting for transfers between devices, by_each_axis(): return lax.psum(half, other)  77.7 us
    dot_general x6, matrix products, factor_forward(): lax.dot_general(ours, block, (((1,), (1,)), ((), ())), precision=highest,...  57 us
    psum x6, blocking collectives, factor_backward(): summed = lax.psum(partial_cols, 'blk')  45.4 us
    dot_general x16, matrix products, kernel_tile(): lax.dot_general(rows_x, centre_x, (((1,), (1,)), ((), ())), preferred_ele...  39.3 us
  transfers between devices with their start and end apart: 12, of which 10 were waited for; matrix products, arithmetic and copies ran while one was open for 4% of the time, Pallas kernels for 0%

profile of v1, /device:TPU:0, one launch (start us, length us, event | category | flops | bytes accessed | tf_op | source)
XLA Modules:
  0.0 1220.0 jit_solution(7724371790776895915)
XLA Ops:
  10.9 12.9 %scatter_fusion.1 = bf16[16,32]{1,0:T(8,128)(2,1)S(1)} fusion(bf16[16,32]{1,0:T(8,128)(2,1)S(1)} %broadcast_in_dim.21, s32[256]{0:T(256)S(1)} %bitcast.127, bf16[256]{0:T(256)(128)(2,1)S(1)} %add_convert_fusion), kind=kCustom, calls=%fused_computation.1 | custom fusion | bytes 3584 | tf_op jit(solution)/shard_map/scatter | solution.py:79
  24.5 7.4 all-to-all-start.1
  32.5 27.0 %scatter_fusion = bf16[16,32,128]{2,1,0:T(8,128)(2,1)} fusion(bf16[16,32,128]{2,1,0:T(8,128)(2,1)} %broadcast_in_dim.20, s32[256]{0:T(256)S(1)} %bitcast.128, bf16[256,128]{1,0:T(8,128)(2,1)S(1)} %copy-done.5), kind=kCustom, calls=%fused_computation | custom fusion | bytes 198656 | tf_op jit(solution)/shard_map/scatter | solution.py:75
  59.5 5.8 all-to-all-start
  65.6 2.9 fusion.63
  68.5 4.8 all-to-all-done
  73.3 9.2 while.44
  83.3 86.5 %all-reduce.10.cloned.1.call-done = f32[7,8192]{1,0:T(8,128)} async-done(((f32[7,8192]{1,0:T(8,128)}), f32[7,8192]{1,0:T(8,128)}) %all-reduce.10.cloned.1.call-update) | async-done | bytes 229392 | tf_op jit(solution)/shard_map/psum | solution.py:15
  169.8 25.9 %all-reduce.12.cloned.1.call-done = f32[7,8192]{1,0:T(8,128)} async-done(((f32[7,8192]{1,0:T(8,128)}), f32[7,8192]{1,0:T(8,128)}) %all-reduce.12.cloned.1.call-update) | async-done | bytes 229392 | tf_op jit(solution)/shard_map/psum | solution.py:16
  195.8 5.7 fusion.68
  201.4 6.9 psum.128
  208.4 22.3 %all_gather.40 = f32[7,8192]{1,0:T(8,128)S(1)} all-gather(f32[7,512]{1,0:T(8,128)S(1)} %psum.128), channel_id=1, replica_groups=mesh['blk'=2,'rows'=16] {'rows'}, dimensions={1}, use_global_device_ids=true | all-gather | bytes 243712 | tf_op jit(solution)/shard_map/all_gather | solution.py:57
  230.7 5.7 fusion.69
  236.4 8.1 psum.129
  244.5 17.8 %all_gather.41 = f32[7,8192]{1,0:T(8,128)S(1)} all-gather(f32[7,512]{1,0:T(8,128)S(1)} %psum.129), channel_id=1, replica_groups=mesh['blk'=2,'rows'=16] {'rows'}, dimensions={1}, use_global_device_ids=true | all-gather | bytes 243712 | tf_op jit(solution)/shard_map/all_gather | solution.py:57
  262.3 9.8 fusion.94
  272.2 84.9 %all-reduce.14.cloned.1.call-done = f32[7,4096]{1,0:T(8,128)} async-done(((f32[7,4096]{1,0:T(8,128)}), f32[7,4096]{1,0:T(8,128)}) %all-reduce.14.cloned.1.call-update) | async-done | bytes 114704 | tf_op jit(solution)/shard_map/psum | solution.py:48
  357.1 7.1 all_gather.42
  364.2 9.1 fusion.87
  373.3 58.7 %psum.131 = bf16[7,4096]{1,0:T(8,128)(2,1)S(1)} all-reduce(f32[7,4096]{1,0:T(8,128)S(1)} %fusion.87), channel_id=1, replica_groups=mesh['blk'=2,'rows'=16] {'rows'}, use_global_device_ids=true, to_apply=%region_13.14 | all-reduce | flops 28672 | bytes 172032 | tf_op jit(solution)/shard_map/psum | solution.py:48
  432.0 4.9 all_gather.43
  436.9 28.1 %while.45 = (s32[]{:T(128)}, f32[7,8192]{1,0:T(8,128)S(1)}, bf16[8,64,128]{2,1,0:T(8,128)(2,1)S(1)}, f32[8192]{0:T(1024)S(1)}, bf16[8192,128]{1,0:T(8,128)(2,1)}...) while((s32[]{:T(128)}, f32[7,8192]{1,0:T(8,128)S(1)}, ...), condition=%wide.region_15.16_spmd.clone, body=%wide.region_14.15_spmd.clone.sunk | while | flops 152183616 | bytes 4834931 | solution.py:111
  437.0 2.5 fusion.178
  440.5 2.5 fusion.178
  444.0 2.5 fusion.178
  447.6 2.5 fusion.178
  451.1 2.5 fusion.178
  458.1 2.5 fusion.178
  465.8 86.1 %all-reduce.16.cloned.1.call-done = f32[7,8192]{1,0:T(8,128)} async-done(((f32[7,8192]{1,0:T(8,128)}), f32[7,8192]{1,0:T(8,128)}) %all-reduce.16.cloned.1.call-update) | async-done | bytes 229392 | tf_op jit(solution)/shard_map/psum | solution.py:15
  551.9 25.9 %all-reduce.18.cloned.1.call-done = f32[7,8192]{1,0:T(8,128)} async-done(((f32[7,8192]{1,0:T(8,128)}), f32[7,8192]{1,0:T(8,128)}) %all-reduce.18.cloned.1.call-update) | async-done | bytes 229392 | tf_op jit(solution)/shard_map/psum | solution.py:16
  577.8 5.7 fusion.67
  583.5 6.9 psum.134
  590.4 22.3 %all_gather.44 = f32[7,8192]{1,0:T(8,128)S(1)} all-gather(f32[7,512]{1,0:T(8,128)S(1)} %psum.134), channel_id=1, replica_groups=mesh['blk'=2,'rows'=16] {'rows'}, dimensions={1}, use_global_device_ids=true | all-gather | bytes 243712 | tf_op jit(solution)/shard_map/all_gather | solution.py:57
  612.7 5.7 fusion.66
  618.4 8.1 psum.135
  626.6 18.0 %all_gather.45 = f32[7,8192]{1,0:T(8,128)S(1)} all-gather(f32[7,512]{1,0:T(8,128)S(1)} %psum.135), channel_id=1, replica_groups=mesh['blk'=2,'rows'=16] {'rows'}, dimensions={1}, use_global_device_ids=true | all-gather | bytes 243712 | tf_op jit(solution)/shard_map/all_gather | solution.py:57
  645.2 9.8 fusion.91
  655.1 84.9 %all-reduce.20.cloned.1.call-done = f32[7,4096]{1,0:T(8,128)} async-done(((f32[7,4096]{1,0:T(8,128)}), f32[7,4096]{1,0:T(8,128)}) %all-reduce.20.cloned.1.call-update) | async-done | bytes 114704 | tf_op jit(solution)/shard_map/psum | solution.py:48
  740.0 6.6 all_gather.46
  746.6 9.1 fusion.84
  755.7 58.7 %psum.137 = bf16[7,4096]{1,0:T(8,128)(2,1)S(1)} all-reduce(f32[7,4096]{1,0:T(8,128)S(1)} %fusion.84), channel_id=1, replica_groups=mesh['blk'=2,'rows'=16] {'rows'}, use_global_device_ids=true, to_apply=%region_23.24 | all-reduce | flops 28672 | bytes 172032 | tf_op jit(solution)/shard_map/psum | solution.py:48
  814.4 4.9 all_gather.47
  819.3 28.1 %while.46 = (s32[]{:T(128)}, f32[7,8192]{1,0:T(8,128)S(1)}, bf16[8,64,128]{2,1,0:T(8,128)(2,1)S(1)}, f32[8192]{0:T(1024)S(1)}, bf16[8192,128]{1,0:T(8,128)(2,1)}...) while((s32[]{:T(128)}, f32[7,8192]{1,0:T(8,128)S(1)}, ...), condition=%wide.region_25.26_spmd.clone, body=%wide.region_24.25_spmd.clone.sunk | while | flops 152183616 | bytes 4834931 | solution.py:111
  819.4 2.5 fusion.185
  822.9 2.5 fusion.185
  826.4 2.5 fusion.185
  829.9 2.5 fusion.185
  833.5 2.5 fusion.185
  840.5 2.5 fusion.185
  848.2 86.1 %all-reduce.22.cloned.1.call-done = f32[7,8192]{1,0:T(8,128)} async-done(((f32[7,8192]{1,0:T(8,128)}), f32[7,8192]{1,0:T(8,128)}) %all-reduce.22.cloned.1.call-update) | async-done | bytes 229392 | tf_op jit(solution)/shard_map/psum | solution.py:15
  934.4 25.9 %all-reduce.24.cloned.1.call-done = f32[7,8192]{1,0:T(8,128)} async-done(((f32[7,8192]{1,0:T(8,128)}), f32[7,8192]{1,0:T(8,128)}) %all-reduce.24.cloned.1.call-update) | async-done | bytes 229392 | tf_op jit(solution)/shard_map/psum | solution.py:16
  960.3 5.7 fusion.65
  966.0 6.9 psum.140
  972.9 22.3 %all_gather.48 = f32[7,8192]{1,0:T(8,128)S(1)} all-gather(f32[7,512]{1,0:T(8,128)S(1)} %psum.140), channel_id=1, replica_groups=mesh['blk'=2,'rows'=16] {'rows'}, dimensions={1}, use_global_device_ids=true | all-gather | bytes 243712 | tf_op jit(solution)/shard_map/all_gather | solution.py:57
  995.2 5.7 fusion.64
  1000.9 8.4 psum.141
  1009.3 17.8 %all_gather.49 = f32[7,8192]{1,0:T(8,128)S(1)} all-gather(f32[7,512]{1,0:T(8,128)S(1)} %psum.141), channel_id=1, replica_groups=mesh['blk'=2,'rows'=16] {'rows'}, dimensions={1}, use_global_device_ids=true | all-gather | bytes 243712 | tf_op jit(solution)/shard_map/all_gather | solution.py:57
  1027.3 9.8 fusion.81
  1037.2 84.9 %all-reduce.26.cloned.1.call-done = f32[7,4096]{1,0:T(8,128)} async-done(((f32[7,4096]{1,0:T(8,128)}), f32[7,4096]{1,0:T(8,128)}) %all-reduce.26.cloned.1.call-update) | async-done | bytes 114704 | tf_op jit(solution)/shard_map/psum | solution.py:48
  1122.1 6.6 all_gather.50
  1128.7 9.3 fusion.79
  1138.0 58.7 %psum.143 = bf16[7,4096]{1,0:T(8,128)(2,1)S(1)} all-reduce(f32[7,4096]{1,0:T(8,128)S(1)} %fusion.79), channel_id=1, replica_groups=mesh['blk'=2,'rows'=16] {'rows'}, use_global_device_ids=true, to_apply=%region_32.33 | all-reduce | flops 28672 | bytes 172032 | tf_op jit(solution)/shard_map/psum | solution.py:48
  1196.6 4.9 all_gather.51
  1201.6 10.7 while.43
  (149 shorter events, 55.7 us)
Async XLA Ops:
  6.5 26.0 %copy-start.5 = (bf16[256,128]{1,0:T(8,128)(2,1)S(1)}, bf16[256,128]{1,0:T(8,128)(2,1)}, u32[]{:S(2)}) copy-start(bf16[256,128]{1,0:T(8,128)(2,1)} %param.14) | copy-start | bytes 196612
  6.5 59.1 %all-gather.2.cloned.1.call-start = ((), (), s32[]{:S(2)}) async-start(), calls=%async_computation.2 | async-start | bytes 3145728 | tf_op jit(solution)/shard_map/all_gather | solution.py:89
  24.5 35.1 %all-to-all-start.1 = ((bf16[16,1,32]{2,1,0:T(2,128)(2,1)}), bf16[16,1,32]{2,1,0:T(2,128)(2,1)S(1)}, u32[]{:S(2)}, u32[]{:S(2)}) async-start(bf16[16,1,32]{2,1,0:T(2,128)(2,1)} %copy.11), calls=%async_computation.1 | async-start | bytes 16384 | tf_op jit(solution)/shard_map/all_to_all | solution.py:83
  59.5 13.8 %all-to-all-start = ((bf16[16,32,128]{2,1,0:T(8,128)(2,1)}), bf16[16,32,128]{2,1,0:T(8,128)(2,1)S(1)}, u32[]{:S(2)}, u32[]{:S(2)}) async-start(bf16[16,32,128]{2,1,0:T(8,128)(2,1)} %scatter_fusion), calls=%async_computation | async-start | bytes 262144 | tf_op jit(solution)/shard_map/all_to_all | solution.py:82
  65.4 104.4 %all-reduce.10.cloned.1.call-start = ((), (), s32[]{:S(2)}) async-start(), calls=%async_computation.3 | async-start | bytes 524288 | tf_op jit(solution)/shard_map/psum | solution.py:15
  65.6 7.7 copy-start.2
  82.5 0.7 copy-start.4
  83.2 112.5 %all-reduce.12.cloned.1.call-start = ((), (), s32[]{:S(2)}) async-start(), calls=%async_computation.4 | async-start | bytes 524288 | tf_op jit(solution)/shard_map/psum | solution.py:16
  169.8 187.3 %all-reduce.14.cloned.1.call-start = ((), (), s32[]{:S(2)}) async-start(), calls=%async_computation.5 | async-start | bytes 262144 | tf_op jit(solution)/shard_map/psum | solution.py:48
  272.1 279.7 %all-reduce.16.cloned.1.call-start = ((), (), s32[]{:S(2)}) async-start(), calls=%async_computation.6 | async-start | bytes 524288 | tf_op jit(solution)/shard_map/psum | solution.py:15
  465.0 0.7 copy-start
  465.7 112.1 %all-reduce.18.cloned.1.call-start = ((), (), s32[]{:S(2)}) async-start(), calls=%async_computation.7 | async-start | bytes 524288 | tf_op jit(solution)/shard_map/psum | solution.py:16
  551.9 188.1 %all-reduce.20.cloned.1.call-start = ((), (), s32[]{:S(2)}) async-start(), calls=%async_computation.8 | async-start | bytes 262144 | tf_op jit(solution)/shard_map/psum | solution.py:48
  655.0 279.3 %all-reduce.22.cloned.1.call-start = ((), (), s32[]{:S(2)}) async-start(), calls=%async_computation.9 | async-start | bytes 524288 | tf_op jit(solution)/shard_map/psum | solution.py:15
  847.4 0.7 copy-start.1
  848.1 112.2 %all-reduce.24.cloned.1.call-start = ((), (), s32[]{:S(2)}) async-start(), calls=%async_computation.10 | async-start | bytes 524288 | tf_op jit(solution)/shard_map/psum | solution.py:16
  934.3 187.7 %all-reduce.26.cloned.1.call-start = ((), (), s32[]{:S(2)}) async-start(), calls=%async_computation.11 | async-start | bytes 262144 | tf_op jit(solution)/shard_map/psum | solution.py:48
  1128.7 72.9 %copy-start.3 = (bf16[8192,128]{1,0:T(8,128)(2,1)S(1)}, bf16[8192,128]{1,0:T(8,128)(2,1)}, u32[]{:S(2)}) copy-start(bf16[8192,128]{1,0:T(8,128)(2,1)} %get-tuple-element.548) | copy-start | bytes 6291460
Sparse Core Ops, SparseCore 0:
  8.9 35.8 all-gather.1
  83.4 86.3 all-reduce.9
  172.0 23.6 all-reduce.11
  272.3 84.7 all-reduce.13
  465.8 85.9 all-reduce.15
  554.1 23.6 all-reduce.17
  655.1 84.7 all-reduce.19
  848.2 86.0 all-reduce.21
  936.6 23.6 all-reduce.23
  1037.2 84.7 all-reduce.25
